TPU v7x, 32 devices: a whole 2x2x4 slice. The times are simulated.
32 devices in a mesh: section: 2 (over y), node: 4 (over z), lane: 4 (over x, core).
Axes of the slice: x: 2, y: 2, z: 4, core: 2. Of those that a mesh axis runs over, the one named last changes fastest.
Arguments:
- forward_input: bfloat16 [2, 1024, 2048], P('section', ('node', 'lane')), may hold values from -6 to 6
- forward_routes: int32 [2, 1024, 8], P('section', ('node', 'lane')), may hold values from 0 to 15, all different within a row; in each aligned block of 64 rows (0 to 63, 64 to 127, ..., all dimensions but the last counted through in order) at most 36 rows name the same one
- forward_gates: float32 [2, 1024, 8], P('section', ('node', 'lane')), may hold values from 0.05 to 0.4
- backward_input: bfloat16 [2, 1024, 2048], P('section', ('node', 'lane')), may hold values from -6 to 6
- backward_cotangent: bfloat16 [2, 1024, 2048], P('section', ('node', 'lane')), may hold values from -6 to 6
- backward_routes: int32 [2, 1024, 8], P('section', ('node', 'lane')), may hold values from 0 to 15, all different within a row; in each aligned block of 64 rows (0 to 63, 64 to 127, ..., all dimensions but the last counted through in order) at most 36 rows name the same one
- backward_gates: float32 [2, 1024, 8], P('section', ('node', 'lane')), may hold values from 0.05 to 0.4
- w_gate: bfloat16 [2, 16, 2048, 768], P('section', ('node', 'lane')), may hold values from -0.125 to 0.125
- w_up: bfloat16 [2, 16, 2048, 768], P('section', ('node', 'lane')), may hold values from -0.125 to 0.125
- w_down: bfloat16 [2, 16, 768, 2048], P('section', ('node', 'lane')), may hold values from -0.21875 to 0.21875
Outputs:
- next_input: bfloat16 [2, 1024, 2048], P('section', ('node', 'lane'))
- previous_gradient: bfloat16 [2, 1024, 2048], P('section', ('node', 'lane'))
Inputs may be any that keep to these rules, and one draw needn't show every extreme that they name: `forward_routes`: each row names 8 different experts. Within the 64 rows of one device (aligned blocks), no expert is named by more than 36 rows, a bound that some block reaches. `backward_routes`: each row names 8 different experts. Within the 64 rows of one device (aligned blocks), no expert is named by more than 36 rows, a bound that some block reaches.
All inputs are finite; a program needn't handle non-finite values.
Results may differ from a plain program's by a relative error of at most 0.0064.
Values may be sent and summed in bfloat16 or wider, within the bound.
A program may use at most 128 MiB of HBM per device.

v0:
```python
import jax
import jax.numpy as jnp
from jax import lax
from jax.sharding import PartitionSpec as P

GROUP = ("node", "lane")


def from_behind(value, axis, steps):
    count = lax.axis_size(axis)
    pairs = [(source, (source + steps) % count) for source in range(count)]
    return lax.ppermute(value, axis, pairs)


def coefficients(routes, gates, experts):
    hit = routes[:, :, None] == jnp.arange(experts, dtype=jnp.int32)[None, None, :]
    return jnp.sum(jnp.where(hit, gates[:, :, None], 0.0), axis=1)


def contract_last(a, b):
    return lax.dot_general(a, b, (((1,), (1,)), ((), ())), preferred_element_type=jnp.float32)


def local(
    forward_input,
    forward_routes,
    forward_gates,
    backward_input,
    backward_cotangent,
    backward_routes,
    backward_gates,
    w_gate,
    w_up,
    w_down,
):
    experts = lax.axis_size("node") * lax.axis_size("lane") * w_gate.shape[1]
    w_g, w_u, w_d = w_gate[0, 0], w_up[0, 0], w_down[0, 0]
    me = lax.axis_index(GROUP)

    coef = jnp.concatenate(
        [
            coefficients(forward_routes[0], forward_gates[0], experts),
            coefficients(backward_routes[0], backward_gates[0], experts),
        ],
        axis=1,
    )
    coef = lax.all_gather(coef, GROUP, axis=0, tiled=True)
    fwd_coef = lax.dynamic_slice_in_dim(coef, me, 1, axis=1)
    bwd_coef = lax.dynamic_slice_in_dim(coef, experts + me, 1, axis=1)

    fwd = lax.all_gather(forward_input[0], GROUP, axis=0, tiled=True)
    bwd = lax.all_gather(backward_input[0], GROUP, axis=0, tiled=True)
    cot = lax.all_gather(backward_cotangent[0], GROUP, axis=0, tiled=True)

    pre_gate = jnp.dot(fwd, w_g, preferred_element_type=jnp.float32)
    pre_up = jnp.dot(fwd, w_u, preferred_element_type=jnp.float32)
    hidden = (jax.nn.silu(pre_gate) * pre_up).astype(jnp.bfloat16)
    out = jnp.dot(hidden, w_d, preferred_element_type=jnp.float32)
    out = (out * fwd_coef).astype(jnp.bfloat16)
    layer_out = lax.psum_scatter(out, GROUP, scatter_dimension=0, tiled=True)

    pre_gate = jnp.dot(bwd, w_g, preferred_element_type=jnp.float32)
    pre_up = jnp.dot(bwd, w_u, preferred_element_type=jnp.float32)
    scaled = (bwd_coef * cot.astype(jnp.float32)).astype(jnp.bfloat16)
    grad_hidden = contract_last(scaled, w_d)
    sigma = jax.nn.sigmoid(pre_gate)
    grad_gate = (grad_hidden * pre_up * sigma * (1.0 + pre_gate * (1.0 - sigma))).astype(
        jnp.bfloat16
    )
    grad_up = (grad_hidden * pre_gate * sigma).astype(jnp.bfloat16)
    total = contract_last(grad_gate, w_g) + contract_last(grad_up, w_u)
    input_grad = lax.psum_scatter(
        total.astype(jnp.bfloat16), GROUP, scatter_dimension=0, tiled=True
    )
    next_input = from_behind(layer_out, "section", 1)
    previous_gradient = from_behind(input_grad, "section", -1)
    return (next_input[None], previous_gradient[None])


def solution(mesh):
    rows = P("section", GROUP, None)
    weights = P("section", GROUP, None, None)
    return jax.shard_map(
        local,
        mesh=mesh,
        in_specs=(rows,) * 7 + (weights,) * 3,
        out_specs=(rows, rows),
        check_vma=False,
    )
```

profile of v0, /device:TPU:0, one launch (start us, length us, event | category | flops | bytes accessed | tf_op | source)
XLA Modules:
  0.0 331.4 jit_solution(10402950304157957264)
XLA Ops:
  7.2 0.0 copy-start
  7.2 0.0 all-gather.12.cloned.1.call-start
  7.2 0.7 all-gather.12.cloned.1.call-update
  7.9 0.0 all-gather.10.cloned.1.call-start
  8.0 0.7 all-gather.10.cloned.1.call-update
  8.7 0.0 all-gather.8.cloned.1.call-start
  8.7 0.7 all-gather.8.cloned.1.call-update
  9.4 0.0 reduce-scatter.5.cloned.1.call-start
  9.5 0.8 select_reduce_fusion
  10.2 24.1 %all-gather.3 = f32[16,64,32]{1,2,0:T(8,128)S(1)} all-gather(f32[1,64,32]{1,2,0:T(8,128)S(1)} %maximum_bitcast_fusion), channel_id=1, replica_groups=mesh['section'=2,'node'=4,'lane'=4] {'node','lane'}, dimensions={0}, use_global_device_ids=true | all-gather | bytes 139264 | tf_op jit(solution)/shard_map/all_gather | solution.py:47
  34.4 0.2 copy.29
  34.5 0.1 reshape.13
  34.7 29.2 %all-gather.12.cloned.1.call-done = bf16[1,1024,2048]{2,1,0:T(8,128)(2,1)} async-done(((bf16[1,64,2048]{2,1,0:T(8,128)(2,1)}), bf16[1,1024,2048]{2,1,0:T(8,128)(2,1)}) %all-gather.12.cloned.1.call-update) | async-done | bytes 4194320 | tf_op jit(solution)/shard_map/all_gather | solution.py:52
  63.9 8.2 %fusion.4 = f32[1024,768]{1,0:T(8,128)} fusion(bf16[1,1024,2048]{2,1,0:T(8,128)(2,1)} %all-gather.12.cloned.1.call-done, bf16[1,1,2048,768]{3,2,1,0:T(8,128)(2,1)} %param.17), kind=kOutput, calls=%fused_computation.6 | convolution fusion | flops 3221225472 | bytes 10485760 | tf_op jit(solution)/shard_map/dot_general | solution.py:62
  72.1 42.9 %all-gather.10.cloned.1.call-done = bf16[1,1024,2048]{2,1,0:T(8,128)(2,1)} async-done(((bf16[1,64,2048]{2,1,0:T(8,128)(2,1)}), bf16[1,1024,2048]{2,1,0:T(8,128)(2,1)}) %all-gather.10.cloned.1.call-update) | async-done | bytes 4194320 | tf_op jit(solution)/shard_map/all_gather | solution.py:53
  115.0 8.3 %fusion.1 = f32[1024,768]{1,0:T(8,128)} fusion(bf16[1,1024,2048]{2,1,0:T(8,128)(2,1)} %all-gather.10.cloned.1.call-done, f32[1024]{0:T(1024)S(1)} %bitcast.66, bf16[1,1,768,2048]{3,2,1,0:T(8,128)(2,1)} %param.19), kind=kOutput, calls=%fused_computation.4 | convolution fusion | flops 3227516928 | bytes 10489856 | tf_op jit(solution)/shard_map/dot_general | solution.py:21
  123.3 0.0 copy-done
  123.3 14.0 %fusion.18 = f32[1024,2048]{1,0:T(8,128)} fusion(bf16[1,1,2048,768]{3,2,1,0:T(8,128)(2,1)} %param.17, f32[1024,768]{1,0:T(8,128)} %fusion.4, f32[1024,768]{1,0:T(8,128)} %fusion.1, bf16[1,1,2048,768]{3,2,1,0:T(8,128)(2,1)S(1)} %copy-done, bf16[1,1024,2048]{2,1,0:T(8,128)(2,1)} %all-gather.12.cloned.1.call-done), kind=kOutput, calls=%fused_computation.20 | convolution fusion | flops 6450315264 | bytes 25165824 | tf_op jit(solution)/shard_map/dot_general | solution.py:21
  137.3 9.2 %add_convert_fusion = bf16[1024,2048]{1,0:T(8,128)(2,1)} fusion(f32[1024,2048]{1,0:T(8,128)} %fusion.18, bf16[1,1,2048,768]{3,2,1,0:T(8,128)(2,1)S(1)} %copy-done, f32[1024,768]{1,0:T(8,128)} %fusion.1, f32[1024,768]{1,0:T(8,128)} %fusion.4), kind=kOutput, calls=%fused_computation.2 | convolution fusion | flops 3230138368 | bytes 22020096 | tf_op jit(solution)/shard_map/dot_general | solution.py:21
  146.5 0.0 reduce-scatter.5.cloned.1.call-update
  146.5 0.2 reduce-scatter.3.cloned.1.call-start
  146.8 19.3 %all-gather.8.cloned.1.call-done = bf16[1,1024,2048]{2,1,0:T(8,128)(2,1)} async-done(((bf16[1,64,2048]{2,1,0:T(8,128)(2,1)}), bf16[1,1024,2048]{2,1,0:T(8,128)(2,1)}) %all-gather.8.cloned.1.call-update) | async-done | bytes 4194320 | tf_op jit(solution)/shard_map/all_gather | solution.py:51
  166.1 8.2 %fusion.10 = f32[1024,768]{1,0:T(8,128)} fusion(bf16[1,1024,2048]{2,1,0:T(8,128)(2,1)} %all-gather.8.cloned.1.call-done, bf16[1,1,2048,768]{3,2,1,0:T(8,128)(2,1)} %param.17), kind=kOutput, calls=%fused_computation.12 | convolution fusion | flops 3221225472 | bytes 10485760 | tf_op jit(solution)/shard_map/dot_general | solution.py:55
  174.4 12.6 %multiply_convert_fusion = bf16[1024,2048]{1,0:T(8,128)(2,1)} fusion(f32[1024]{0:T(1024)S(1)} %bitcast.65, bf16[1,1,768,2048]{3,2,1,0:T(8,128)(2,1)} %param.19, f32[1024,768]{1,0:T(8,128)} %fusion.10, bf16[1,1,2048,768]{3,2,1,0:T(8,128)(2,1)S(1)} %copy-done, bf16[1,1024,2048]{2,1,0:T(8,128)(2,1)} %all-gather.8.cloned.1.call-done), kind=kOutput, calls=%fused_computation.3 | convolution fusion | flops 6451363840 | bytes 17829888 | tf_op jit(solution)/shard_map/dot_general | solution.py:58
  187.0 0.0 reduce-scatter.3.cloned.1.call-update
  187.0 54.2 %reduce-scatter.5.cloned.1.call-done = bf16[64,2048]{1,0:T(8,128)(2,1)} async-done(((bf16[1024,2048]{1,0:T(8,128)(2,1)}), bf16[64,2048]{1,0:T(8,128)(2,1)}) %reduce-scatter.5.cloned.1.call-update) | async-done | bytes 262160 | tf_op jit(solution)/shard_map/reduce_scatter | solution.py:72
  241.2 1.5 collective-permute-start.1
  242.6 74.1 %reduce-scatter.3.cloned.1.call-done = bf16[64,2048]{1,0:T(8,128)(2,1)} async-done(((bf16[1024,2048]{1,0:T(8,128)(2,1)}), bf16[64,2048]{1,0:T(8,128)(2,1)}) %reduce-scatter.3.cloned.1.call-update) | async-done | bytes 262160 | tf_op jit(solution)/shard_map/reduce_scatter | solution.py:60
  316.7 1.4 collective-permute-start
  318.2 0.0 collective-permute-done.1
  318.2 5.3 %collective-permute-done = bf16[64,2048]{1,0:T(8,128)(2,1)S(1)} collective-permute-done((bf16[64,2048]{1,0:T(8,128)(2,1)}, bf16[64,2048]{1,0:T(8,128)(2,1)S(1)}, u32[]{:S(2)}, u32[]{:S(2)}) %collective-permute-start) | collective-permute-done | bytes 262176 | tf_op jit(solution)/shard_map/ppermute | solution.py:12
  323.5 0.7 copy.32
  324.2 0.7 copy.33
  (2 shorter events, 0.0 us)
Async XLA Ops:
  7.2 116.2 %copy-start = (bf16[1,1,2048,768]{3,2,1,0:T(8,128)(2,1)S(1)}, bf16[1,1,2048,768]{3,2,1,0:T(8,128)(2,1)}, u32[]{:S(2)}) copy-start(bf16[1,1,2048,768]{3,2,1,0:T(8,128)(2,1)} %param.18) | copy-start | bytes 9437188
  7.2 56.7 %all-gather.12.cloned.1.call-start = ((), (), s32[]{:S(2)}) async-start(), calls=%async_computation.6 | async-start | bytes 4456448 | tf_op jit(solution)/shard_map/all_gather | solution.py:52
  7.9 107.1 %all-gather.10.cloned.1.call-start = ((), (), s32[]{:S(2)}) async-start(), calls=%async_computation.5 | async-start | bytes 4456448 | tf_op jit(solution)/shard_map/all_gather | solution.py:53
  8.7 157.4 %all-gather.8.cloned.1.call-start = ((), (), s32[]{:S(2)}) async-start(), calls=%async_computation.4 | async-start | bytes 4456448 | tf_op jit(solution)/shard_map/all_gather | solution.py:51
  9.4 231.8 %reduce-scatter.5.cloned.1.call-start = ((), (), s32[]{:S(2)}) async-start(), calls=%async_computation.3 | async-start | bytes 4456448 | tf_op jit(solution)/shard_map/reduce_scatter | solution.py:72
  146.5 170.2 %reduce-scatter.3.cloned.1.call-start = ((), (), s32[]{:S(2)}) async-start(), calls=%async_computation.2 | async-start | bytes 4456448 | tf_op jit(solution)/shard_map/reduce_scatter | solution.py:60
  241.2 77.0 %collective-permute-start.1 = (bf16[64,2048]{1,0:T(8,128)(2,1)}, bf16[64,2048]{1,0:T(8,128)(2,1)S(1)}, u32[]{:S(2)}, u32[]{:S(2)}) collective-permute-start(bf16[64,2048]{1,0:T(8,128)(2,1)} %reduce-scatter.5.cloned.1.call-done), channel_id=1, source_target_pairs={{0,16},{16,0},{1,17},{17,1},{2,18},{18,2},{3,19},{19,3},{4,20},{20... | collective-permute-start | bytes 786440 | tf_op jit(solution)/shard_map/ppermute | solution.py:12
  316.7 6.7 %collective-permute-start = (bf16[64,2048]{1,0:T(8,128)(2,1)}, bf16[64,2048]{1,0:T(8,128)(2,1)S(1)}, u32[]{:S(2)}, u32[]{:S(2)}) collective-permute-start(bf16[64,2048]{1,0:T(8,128)(2,1)} %reduce-scatter.3.cloned.1.call-done), channel_id=1, source_target_pairs={{0,16},{16,0},{1,17},{17,1},{2,18},{18,2},{3,19},{19,3},{4,20},{20... | collective-permute-start | bytes 786440 | tf_op jit(solution)/shard_map/ppermute | solution.py:12
Sparse Core Ops, SparseCore 0:
  10.1 53.6 all-gather.11
  66.0 48.8 all-gather.9
  117.2 48.9 all-gather.7
  169.8 71.2 reduce-scatter.4
  244.9 71.8 reduce-scatter.2
where the time goes:
time: 332 us; the launch traced here: 331 us
  waiting for transfers between devices  227 us (68%)
  matrix products  60.6 us (18%)
  blocking collectives  24.1 us (7%)
  between operations  13.8 us (4%)
    reduce_scatter x1, waiting for transfers between devices, local(): layer_out = lax.psum_scatter(out, GROUP, scatter_dimension=0, tiled=True)  74.1 us
    reduce_scatter x1, waiting for transfers between devices, local(): lax.psum_scatter(total.astype(jnp.bfloat16), GROUP, scatter_dimension=0,...  54.2 us
    all_gather x1, waiting for transfers between devices, local(): cot = lax.all_gather(backward_cotangent[0], GROUP, axis=0, tiled=True)  42.9 us
    dot_general x3, matrix products, contract_last(): lax.dot_general(a, b, (((1,), (1,)), ((), ())), preferred_element_type=jn...  31.5 us
    all_gather x1, waiting for transfers between devices, local(): bwd = lax.all_gather(backward_input[0], GROUP, axis=0, tiled=True)  29.2 us
    all_gather x1, blocking collectives, local(): coef = lax.all_gather(coef, GROUP, axis=0, tiled=True)  24.1 us
    all_gather x1, waiting for transfers between devices, local(): fwd = lax.all_gather(forward_input[0], GROUP, axis=0, tiled=True)  19.3 us
    dot_general x1, matrix products, local(): out = jnp.dot(hidden, w_d, preferred_element_type=jnp.float32)  12.6 us
  transfers between devices with their start and end apart: 7, of which 6 were waited for; matrix products, arithmetic and copies ran while one was open for 19% of the time, Pallas kernels for 0%

commit v1 on v0

--- a/solution.py
+++ b/solution.py
@@ -1,15 +1,372 @@
+import functools
+
 import jax
 import jax.numpy as jnp
 from jax import lax
+from jax.experimental import pallas as pl
+from jax.experimental.pallas import tpu as pltpu
 from jax.sharding import PartitionSpec as P
 
 GROUP = ("node", "lane")
-
-
-def from_behind(value, axis, steps):
-    count = lax.axis_size(axis)
-    pairs = [(source, (source + steps) % count) for source in range(count)]
-    return lax.ppermute(value, axis, pairs)
+CORES = 2
+MESH = pl.DeviceIdType.MESH
+
+
+def position():
+    node, lane = lax.axis_index("node"), lax.axis_index("lane")
+    return node, lane // CORES, lane % CORES
+
+
+def greet(peers):
+    barrier = pltpu.get_barrier_semaphore()
+    for cond, device in peers:
+        @pl.when(cond)
+        def _():
+            pl.semaphore_signal(barrier, inc=1, device_id=device, device_id_type=MESH)
+    pl.semaphore_wait(barrier, sum(jnp.where(cond, 1, 0) for cond, _ in peers))
+
+
+def gather_kernel(n_node, n_x, count, *refs):
+    ins, outs = refs[:count], refs[count : 2 * count]
+    local_sem, recv, z_sem, x_sem, core_sem = refs[2 * count :]
+    node, x, core = position()
+    lane = x * CORES + core
+    z_up, z_down = {"node": node + 1}, {"node": node - 1}
+    x_up, x_down = {"lane": lane + CORES}, {"lane": lane - CORES}
+    partner = {"lane": lane + 1 - 2 * core}
+    has_up, has_down = node < n_node - 1, node > 0
+    has_right, has_left = x < n_x - 1, x > 0
+    greet(
+        [
+            (has_up, z_up),
+            (has_down, z_down),
+            (has_right, x_up),
+            (has_left, x_down),
+            (core < CORES, partner),
+        ]
+    )
+    sends = []
+
+    def send(cond, a, src, z, at_x, sem, device):
+        where = outs[a].at[z, at_x * CORES + core]
+
+        def copy():
+            return pltpu.make_async_remote_copy(
+                src_ref=where if src is None else src,
+                dst_ref=where,
+                send_sem=sem,
+                recv_sem=recv.at[a, z, at_x * CORES + core],
+                device_id=device,
+                device_id_type=MESH,
+            )
+
+        @pl.when(cond)
+        def _():
+            copy().start()
+
+        sends.append((cond, copy))
+
+    def arrived(a, z, at_lane):
+        where = outs[a].at[z, at_lane]
+        pltpu.make_async_remote_copy(
+            src_ref=where,
+            dst_ref=where,
+            send_sem=core_sem.at[a, 0, 0],
+            recv_sem=recv.at[a, z, at_lane],
+            device_id=partner,
+            device_id_type=MESH,
+        ).wait_recv()
+
+    def along_x(cond, a, src, z):
+        send(cond & has_right, a, src, z, x, x_sem.at[a, 0, z, x], x_up)
+        send(cond & has_left, a, src, z, x, x_sem.at[a, 1, z, x], x_down)
+        send(cond, a, src, z, x, core_sem.at[a, z, x], partner)
+
+    always = core < CORES
+    keeps = []
+    for a in range(count):
+        send(has_up, a, ins[a], node, x, z_sem.at[a, 0, node], z_up)
+        send(has_down, a, ins[a], node, x, z_sem.at[a, 1, node], z_down)
+        along_x(always, a, ins[a], node)
+    for a in range(count):
+        keep = pltpu.make_async_copy(ins[a], outs[a].at[node, lane], local_sem.at[a])
+        keep.start()
+        keeps.append(keep)
+    for step in range(1, n_node):
+        for a in range(count):
+            below, above = node - step, node + step
+            from_below, from_above = below >= 0, above < n_node
+
+            @pl.when(from_below)
+            def _():
+                arrived(a, below, lane)
+
+            send(from_below & has_up, a, None, below, x, z_sem.at[a, 0, below], z_up)
+            along_x(from_below, a, None, below)
+
+            @pl.when(from_above)
+            def _():
+                arrived(a, above, lane)
+
+            send(from_above & has_down, a, None, above, x, z_sem.at[a, 1, above], z_down)
+            along_x(from_above, a, None, above)
+    for step in range(1, n_x):
+        for a in range(count):
+            for k in range(n_node):
+                z = (node + k) % n_node
+                for at_x, cond, go_on, way, device in (
+                    (x - step, x - step >= 0, has_right, 0, x_up),
+                    (x + step, x + step < n_x, has_left, 1, x_down),
+                ):
+                    @pl.when(cond)
+                    def _():
+                        arrived(a, z, at_x * CORES + core)
+
+                    if n_x > 2:
+                        send(cond & go_on, a, None, z, at_x, x_sem.at[a, way, z, at_x], device)
+                    send(cond, a, None, z, at_x, core_sem.at[a, z, at_x], partner)
+    for a in range(count):
+        for k in range(n_node):
+            for at_x in range(n_x):
+                arrived(a, k, at_x * CORES + 1 - core)
+    for cond, copy in sends:
+        @pl.when(cond)
+        def _():
+            copy().wait_send()
+    for keep in keeps:
+        keep.wait()
+
+
+def gather(*arrays):
+    n_node, n_lane = lax.axis_size("node"), lax.axis_size("lane")
+    n_x, count = n_lane // CORES, len(arrays)
+    return pl.pallas_call(
+        functools.partial(gather_kernel, n_node, n_x, count),
+        out_shape=[jax.ShapeDtypeStruct((n_node, n_lane) + a.shape, a.dtype) for a in arrays],
+        in_specs=[pl.BlockSpec(memory_space=pltpu.VMEM)] * count,
+        out_specs=[pl.BlockSpec(memory_space=pl.ANY)] * count,
+        scratch_shapes=[
+            pltpu.SemaphoreType.DMA((count,)),
+            pltpu.SemaphoreType.DMA((count, n_node, n_lane)),
+            pltpu.SemaphoreType.DMA((count, 2, n_node)),
+            pltpu.SemaphoreType.DMA((count, 2, n_node, n_x)),
+            pltpu.SemaphoreType.DMA((count, n_node, n_x)),
+        ],
+        compiler_params=pltpu.CompilerParams(collective_id=0, has_side_effects=True),
+    )(*arrays)
+
+
+def scatter_kernel(n_section, n_node, n_x, count, *refs):
+    parts, outs = refs[:count], refs[count : 2 * count]
+    (own, core_in, x_in, z_in, final, local_sem, core_send, core_recv, x_send, x_recv, z_send,
+     z_recv, y_send, y_recv) = refs[2 * count :]
+    node, x, core = position()
+    section = lax.axis_index("section")
+    lane = x * CORES + core
+    partner = {"lane": lane + 1 - 2 * core}
+    z_up, z_down = {"node": node + 1}, {"node": node - 1}
+    x_up, x_down = {"lane": lane + CORES}, {"lane": lane - CORES}
+    after = {"section": (section + 1) % n_section}
+    before = {"section": (section + n_section - 1) % n_section}
+    has_up, has_down = node < n_node - 1, node > 0
+    has_right, has_left = x < n_x - 1, x > 0
+    always = core < CORES
+    greet(
+        [
+            (has_up, z_up),
+            (has_down, z_down),
+            (has_right, x_up),
+            (has_left, x_down),
+            (always, partner),
+            (always, after),
+            (always, before),
+        ]
+    )
+
+    def remote(src, dst, send_sem, recv_sem, device):
+        return pltpu.make_async_remote_copy(
+            src_ref=src,
+            dst_ref=dst,
+            send_sem=send_sem,
+            recv_sem=recv_sem,
+            device_id=device,
+            device_id_type=MESH,
+        )
+
+    def add(target, *others):
+        total = target[...].astype(jnp.float32)
+        for other in others:
+            total = total + other[...].astype(jnp.float32)
+        target[...] = total.astype(target.dtype)
+
+    sends = []
+
+    def start(cond, make):
+        @pl.when(cond)
+        def _():
+            make().start()
+
+        sends.append((cond, make))
+
+    owners = []
+    for t in range(n_node - 1):
+        owners.append((node + n_node - 1 - t, t >= node))
+        owners.append((t + node - (n_node - 1), t + node >= n_node - 1))
+    x_steps = [
+        (t, x + n_x - 1 - t, t >= x, t + x - (n_x - 1), t + x >= n_x - 1) for t in range(n_x - 1)
+    ]
+    every = owners + [(node, always)]
+
+    loads = []
+    for a in range(count):
+        load = pltpu.make_async_copy(parts[a].at[:, :, core], own.at[a], local_sem.at[a])
+        load.start()
+        loads.append(load)
+
+    def core_copy(a, z, at_x):
+        return remote(
+            parts[a].at[z, at_x, 1 - core],
+            core_in.at[a, z, at_x],
+            core_send.at[a, z, at_x],
+            core_recv.at[a, z, at_x],
+            partner,
+        )
+
+    for a in range(count):
+        for z, cond in every:
+            for _, q_up, c_up, q_down, c_down in x_steps:
+                start(cond & c_up, functools.partial(core_copy, a, z, q_up))
+                start(cond & c_down, functools.partial(core_copy, a, z, q_down))
+        for z, cond in every:
+            start(cond, functools.partial(core_copy, a, z, x))
+
+    def x_copy(a, z, q, slot, device):
+        return remote(
+            own.at[a, z, q], x_in.at[a, z, slot], x_send.at[a, z, q], x_recv.at[a, z, slot], device
+        )
+
+    def z_copy(a, z, slot, device):
+        return remote(
+            own.at[a, z, x], z_in.at[a, slot], z_send.at[a, z], z_recv.at[a, slot], device
+        )
+
+    for a in range(count):
+        loads[a].wait()
+        for z, cond in every:
+            for t, q_up, c_up, q_down, c_down in x_steps:
+                for q, c, more, slot, device in (
+                    (q_up, c_up, has_left, q_up, x_up),
+                    (q_down, c_down, has_right, None, x_down),
+                ):
+                    @pl.when(cond & c)
+                    def _():
+                        core_copy(a, z, q).wait_recv()
+                        add(own.at[a, z, q], core_in.at[a, z, q])
+
+                    if t > 0:
+                        @pl.when(cond & c & more)
+                        def _():
+                            x_copy(a, z, q, q, partner).wait_recv()
+                            add(own.at[a, z, q], x_in.at[a, z, q])
+
+                    if slot is not None:
+                        start(cond & c, functools.partial(x_copy, a, z, q, slot, device))
+                    else:
+                        near = q == x - 1
+                        start(
+                            cond & c & near, functools.partial(x_copy, a, z, q, n_x, device)
+                        )
+                        if n_x > 2:
+                            start(
+                                cond & c & (q < x - 1),
+                                functools.partial(x_copy, a, z, q, q, device),
+                            )
+
+    def collect(a, z):
+        core_copy(a, z, x).wait_recv()
+        add(own.at[a, z, x], core_in.at[a, z, x])
+        for c, slot in ((has_left, x), (has_right, n_x)):
+            @pl.when(c)
+            def _():
+                x_copy(a, z, 0, slot, partner).wait_recv()
+                add(own.at[a, z, x], x_in.at[a, z, slot])
+
+    for a in range(count):
+        for k, (z, cond) in enumerate(owners):
+            going_up = k % 2 == 0
+
+            @pl.when(cond)
+            def _():
+                collect(a, z)
+
+            if k >= 2:
+                @pl.when(cond & (has_down if going_up else has_up))
+                def _():
+                    z_copy(a, z, z, partner).wait_recv()
+                    add(own.at[a, z, x], z_in.at[a, z])
+
+            if going_up:
+                start(cond, functools.partial(z_copy, a, z, z, z_up))
+            else:
+                start(cond & (z == node - 1), functools.partial(z_copy, a, z, n_node, z_down))
+                if n_node > 2:
+                    start(cond & (z < node - 1), functools.partial(z_copy, a, z, z, z_down))
+        collect(a, node)
+
+    def y_copy(a):
+        return remote(
+            final.at[a], outs[a], y_send.at[a], y_recv.at[a], after if a == 0 else before
+        )
+
+    for a in range(count):
+        for c, slot in ((has_down, node), (has_up, n_node)):
+            @pl.when(c)
+            def _():
+                z_copy(a, node, slot, partner).wait_recv()
+                add(own.at[a, node, x], z_in.at[a, slot])
+        final[a] = own[a, node, x]
+        y_copy(a).start()
+    for a in range(count):
+        y_copy(a).wait()
+    for cond, make in sends:
+        @pl.when(cond)
+        def _():
+            make().wait_send()
+
+
+def scatter(*parts):
+    n_section, n_node = lax.axis_size("section"), lax.axis_size("node")
+    n_x, count = lax.axis_size("lane") // CORES, len(parts)
+    rows, width = parts[0].shape
+    tok = rows // (n_node * n_x * CORES)
+    dtype = parts[0].dtype
+    block = (tok, width)
+    dma = pltpu.SemaphoreType.DMA
+    return pl.pallas_call(
+        functools.partial(scatter_kernel, n_section, n_node, n_x, count),
+        out_shape=[jax.ShapeDtypeStruct(block, dtype)] * count,
+        in_specs=[pl.BlockSpec(memory_space=pl.ANY)] * count,
+        out_specs=[pl.BlockSpec(memory_space=pltpu.VMEM)] * count,
+        scratch_shapes=[
+            pltpu.VMEM((count, n_node, n_x) + block, dtype),
+            pltpu.VMEM((count, n_node, n_x) + block, dtype),
+            pltpu.VMEM((count, n_node, n_x + 1) + block, dtype),
+            pltpu.VMEM((count, n_node + 1) + block, dtype),
+            pltpu.VMEM((count,) + block, dtype),
+            dma((count,)),
+            dma((count, n_node, n_x)),
+            dma((count, n_node, n_x)),
+            dma((count, n_node, n_x)),
+            dma((count, n_node, n_x + 1)),
+            dma((count, n_node)),
+            dma((count, n_node + 1)),
+            dma((count,)),
+            dma((count,)),
+        ],
+        compiler_params=pltpu.CompilerParams(
+            collective_id=1, has_side_effects=True, vmem_limit_bytes=67043328
+        ),
+    )(*(part.reshape((n_node, n_x, CORES) + block) for part in parts))
 
 
 def coefficients(routes, gates, experts):
@@ -44,20 +401,20 @@
         ],
         axis=1,
     )
-    coef = lax.all_gather(coef, GROUP, axis=0, tiled=True)
+    coef = jnp.pad(coef, ((0, 0), (0, -coef.shape[1] % 128)))
+    tokens = forward_input.shape[1] * lax.axis_size("node") * lax.axis_size("lane")
+    coef, fwd, bwd, cot = (
+        array.reshape(tokens, -1)
+        for array in gather(coef, forward_input[0], backward_input[0], backward_cotangent[0])
+    )
     fwd_coef = lax.dynamic_slice_in_dim(coef, me, 1, axis=1)
     bwd_coef = lax.dynamic_slice_in_dim(coef, experts + me, 1, axis=1)
-
-    fwd = lax.all_gather(forward_input[0], GROUP, axis=0, tiled=True)
-    bwd = lax.all_gather(backward_input[0], GROUP, axis=0, tiled=True)
-    cot = lax.all_gather(backward_cotangent[0], GROUP, axis=0, tiled=True)
 
     pre_gate = jnp.dot(fwd, w_g, preferred_element_type=jnp.float32)
     pre_up = jnp.dot(fwd, w_u, preferred_element_type=jnp.float32)
     hidden = (jax.nn.silu(pre_gate) * pre_up).astype(jnp.bfloat16)
     out = jnp.dot(hidden, w_d, preferred_element_type=jnp.float32)
     out = (out * fwd_coef).astype(jnp.bfloat16)
-    layer_out = lax.psum_scatter(out, GROUP, scatter_dimension=0, tiled=True)
 
     pre_gate = jnp.dot(bwd, w_g, preferred_element_type=jnp.float32)
     pre_up = jnp.dot(bwd, w_u, preferred_element_type=jnp.float32)
@@ -69,11 +426,7 @@
     )
     grad_up = (grad_hidden * pre_gate * sigma).astype(jnp.bfloat16)
     total = contract_last(grad_gate, w_g) + contract_last(grad_up, w_u)
-    input_grad = lax.psum_scatter(
-        total.astype(jnp.bfloat16), GROUP, scatter_dimension=0, tiled=True
-    )
-    next_input = from_behind(layer_out, "section", 1)
-    previous_gradient = from_behind(input_grad, "section", -1)
+    next_input, previous_gradient = scatter(out, total.astype(jnp.bfloat16))
     return (next_input[None], previous_gradient[None])
 
 

time: 332 us -> 213 us (0.64)
  waiting for transfers between devices: 227 us -> 0 us
  Pallas kernels: 0 us -> 145 us
  blocking collectives: 24.1 us -> 0 us
  between operations: 13.8 us -> 0.68 us
  matrix products: 60.6 us -> 55.9 us
  other arithmetic: 0.77 us -> 5.23 us
  local copies, waits for them, and re-layouts: 1.71 us -> 5.54 us
    pallas_call x0 -> x2, Pallas kernels: none -> 145 us  [the longest x1 79.7 us: gather(): pl.pallas_call(functools.partial(gather_kernel, n_node, n_x, count), out_...]
    reduce_scatter x2 -> x0, waiting for transfers between devices: 128 us -> none  [the longest x1 74.1 us: local(): layer_out = lax.psum_scatter(out, GROUP, scatter_dimension=0, tiled=True)]
    all_gather x3 -> x0, waiting for transfers between devices: 91.4 us -> none  [the longest x1 42.9 us: local(): cot = lax.all_gather(backward_cotangent[0], GROUP, axis=0, tiled=True)]
    all_gather x1 -> x0, blocking collectives: 24.1 us -> none  [local(): coef = lax.all_gather(coef, GROUP, axis=0, tiled=True)]
    ppermute x2 -> x0, waiting for transfers between devices: 5.29 us -> none  [from_behind(): return lax.ppermute(value, axis, pairs)]
    unnamed x5 -> x12, local copies, waits for them, and re-layouts: 1.54 us -> 5.3 us
  transfers between devices with their start and end apart: 7 -> 0, of which waited for: 6 -> 0; matrix products, arithmetic and copies ran while one was open for 19% -> 0% of each run, Pallas kernels for 0% -> 0%
where the time goes in v1:
time: 213 us
  Pallas kernels  145 us (68%)
  matrix products  55.9 us (26%)
  local copies, waits for them, and re-layouts  5.54 us (3%)
  other arithmetic  5.23 us (2%)
    pallas_call x1, Pallas kernels, gather(): pl.pallas_call(functools.partial(gather_kernel, n_node, n_x, count), out_...  79.7 us
    pallas_call x1, Pallas kernels, scatter(): pl.pallas_call(functools.partial(scatter_kernel, n_section, n_node, n_x,...  65.5 us
    dot_general x3, matrix products, contract_last(): lax.dot_general(a, b, (((1,), (1,)), ((), ())), preferred_element_type=jn...  29.2 us
    dot_general x1, matrix products, local(): out = jnp.dot(hidden, w_d, preferred_element_type=jnp.float32)  13.2 us
    dot_general x1, matrix products, local(): pre_gate = jnp.dot(bwd, w_g, preferred_element_type=jnp.float32)  8.39 us
    unnamed x12, local copies, waits for them, and re-layouts  5.3 us
    dot_general x1, matrix products, local(): pre_up = jnp.dot(fwd, w_u, preferred_element_type=jnp.float32)  5.1 us

profile of v1, /device:TPU:0, one launch (start us, length us, event | category | flops | bytes accessed | tf_op | source)
XLA Modules:
  0.0 212.5 jit_solution(11550830617971006731)
XLA Ops:
  0.6 0.7 select_reduce_fusion.1
  1.4 0.7 select_reduce_fusion
  2.1 0.1 copy.23
  2.2 0.1 copy.22
  2.3 0.7 select_maximum_fusion.refs_0_
  2.9 79.7 %shard_map.113 = (f32[4,4,64,128]{3,2,1,0:T(8,128)}, bf16[4,4,64,2048]{3,2,1,0:T(8,128)(2,1)}, bf16[4,4,64,2048]{3,2,1,0:T(8,128)(2,1)}, bf16[4,4,64,2048]{3,2,1,0:T(8,128)(2,1)}) custom-call(f32[64,128]{1,0:T(8,128)} %select_maximum_fusion.refs_0_, bf16[64,2048]{1,0:T(8,128)(2,1)} %bitcast.52, bf16[64,2048]{1,0:T(8,128)(2,1)} %bitcast.53, ...), custom_call_target="tpu_custom_call" | custom-call | tf_op jit(solution)/shard_map/pallas_call | solution.py:143
  82.6 1.7 dynamic-slice_reduce_fusion
  84.3 0.1 mul.55
  84.4 0.0 copy-start.1
  84.4 3.1 %multiply_convert_fusion = bf16[4,4,64,2048]{3,2,1,0:T(8,128)(2,1)S(1)} fusion(bf16[4,4,64,2048]{3,2,1,0:T(8,128)(2,1)} %get-tuple-element.10, f32[4,4,64]{2,1,0:T(4,128)S(1)} %mul.55), kind=kLoop, calls=%fused_computation.1 | loop fusion | flops 6291456 | bytes 8392704 | tf_op jit(solution)/shard_map/convert_element_type | solution.py:421
  87.5 0.1 copy-done.1
  87.6 5.2 %fusion = f32[1024,768]{1,0:T(8,128)} fusion(bf16[1024,2048]{1,0:T(8,128)(2,1)S(1)} %bitcast.48, bf16[1,1,768,2048]{3,2,1,0:T(8,128)(2,1)S(1)} %copy-done.1), kind=kOutput, calls=%fused_computation.3 | convolution fusion | flops 3221225472 | bytes 10485760 | tf_op jit(solution)/shard_map/dot_general | solution.py:378
  92.7 0.2 copy.26
  92.9 0.0 copy-start
  92.9 0.0 copy-start.2
  92.9 8.4 %fusion.10 = f32[1024,768]{1,0:T(8,128)} fusion(bf16[1024,2048]{1,0:T(8,128)(2,1)} %bitcast.62, bf16[1,1,2048,768]{3,2,1,0:T(8,128)(2,1)} %param.17), kind=kOutput, calls=%fused_computation.13 | convolution fusion | flops 3221225472 | bytes 10485760 | tf_op jit(solution)/shard_map/dot_general | solution.py:419
  101.3 0.0 copy-done
  101.3 0.0 copy-done.2
  101.3 5.1 %fusion.6 = f32[1024,768]{1,0:T(8,128)} fusion(bf16[1024,2048]{1,0:T(8,128)(2,1)S(1)} %bitcast.65, bf16[1,1,2048,768]{3,2,1,0:T(8,128)(2,1)S(1)} %copy-done.2), kind=kOutput, calls=%fused_computation.9 | convolution fusion | flops 3221225472 | bytes 10485760 | tf_op jit(solution)/shard_map/dot_general | solution.py:414
  106.4 13.2 %multiply_convert_fusion.1 = bf16[1024,2048]{1,0:T(8,128)(2,1)} fusion(f32[1024]{0:T(1024)S(1)} %bitcast.57, bf16[1,1,768,2048]{3,2,1,0:T(8,128)(2,1)} %param.19, f32[1024,768]{1,0:T(8,128)} %fusion.6, bf16[1024,2048]{1,0:T(8,128)(2,1)} %bitcast.64, bf16[1,1,2048,768]{3,2,1,0:T(8,128)(2,1)} %param.17), kind=kOutput, calls=%fused_computation.2 | convolution fusion | flops 6451363840 | bytes 17829888 | tf_op jit(solution)/shard_map/dot_general | solution.py:416
  119.6 0.0 copy-start.3
  119.6 14.9 %fusion.8 = f32[1024,2048]{1,0:T(8,128)} fusion(bf16[1,1,2048,768]{3,2,1,0:T(8,128)(2,1)} %param.17, f32[1024,768]{1,0:T(8,128)} %fusion.10, f32[1024,768]{1,0:T(8,128)} %fusion, bf16[1024,2048]{1,0:T(8,128)(2,1)} %bitcast.63, bf16[1,1,2048,768]{3,2,1,0:T(8,128)(2,1)} %param.18), kind=kOutput, calls=%fused_computation.11 | convolution fusion | flops 6450315264 | bytes 25165824 | tf_op jit(solution)/shard_map/dot_general | solution.py:378
  134.5 0.0 copy-done.3
  134.5 9.2 %add_convert_fusion = bf16[1024,2048]{1,0:T(8,128)(2,1)} fusion(f32[1024,2048]{1,0:T(8,128)} %fusion.8, bf16[1,1,2048,768]{3,2,1,0:T(8,128)(2,1)S(1)} %copy-done.3, f32[1024,768]{1,0:T(8,128)} %fusion, f32[1024,768]{1,0:T(8,128)} %fusion.10), kind=kOutput, calls=%fused_computation | convolution fusion | flops 3230138368 | bytes 22020096 | tf_op jit(solution)/shard_map/dot_general | solution.py:378
  143.7 65.5 %shard_map.114 = (bf16[64,2048]{1,0:T(8,128)(2,1)}, bf16[64,2048]{1,0:T(8,128)(2,1)}) custom-call(bf16[4,2,2,64,2048]{4,3,2,1,0:T(8,128)(2,1)} %bitcast.49, bf16[4,2,2,64,2048]{4,3,2,1,0:T(8,128)(2,1)} %bitcast.50), custom_call_target="tpu_custom_call" | custom-call | tf_op jit(solution)/shard_map/pallas_call | solution.py:345
  209.2 1.7 copy.31
  210.9 1.7 copy.32
Async XLA Ops:
  84.4 3.2 %copy-start.1 = (bf16[1,1,768,2048]{3,2,1,0:T(8,128)(2,1)S(1)}, bf16[1,1,768,2048]{3,2,1,0:T(8,128)(2,1)}, u32[]{:S(2)}) copy-start(bf16[1,1,768,2048]{3,2,1,0:T(8,128)(2,1)} %param.19) | copy-start | bytes 9437188
  92.9 8.4 %copy-start = (bf16[4,4,64,2048]{3,2,1,0:T(8,128)(2,1)S(1)}, bf16[4,4,64,2048]{3,2,1,0:T(8,128)(2,1)}, u32[]{:S(2)}) copy-start(bf16[4,4,64,2048]{3,2,1,0:T(8,128)(2,1)} %get-tuple-element.8) | copy-start | bytes 12582916
  92.9 8.4 %copy-start.2 = (bf16[1,1,2048,768]{3,2,1,0:T(8,128)(2,1)S(1)}, bf16[1,1,2048,768]{3,2,1,0:T(8,128)(2,1)}, u32[]{:S(2)}) copy-start(bf16[1,1,2048,768]{3,2,1,0:T(8,128)(2,1)} %param.18) | copy-start | bytes 9437188
  119.6 14.9 %copy-start.3 = (bf16[1,1,2048,768]{3,2,1,0:T(8,128)(2,1)S(1)}, bf16[1,1,2048,768]{3,2,1,0:T(8,128)(2,1)}, u32[]{:S(2)}) copy-start(bf16[1,1,2048,768]{3,2,1,0:T(8,128)(2,1)} %param.18) | copy-start | bytes 9437188

commit v2 on v1

--- a/solution.py
+++ b/solution.py
@@ -413,18 +413,19 @@
     pre_gate = jnp.dot(fwd, w_g, preferred_element_type=jnp.float32)
     pre_up = jnp.dot(fwd, w_u, preferred_element_type=jnp.float32)
     hidden = (jax.nn.silu(pre_gate) * pre_up).astype(jnp.bfloat16)
+    hidden = lax.optimization_barrier(hidden)
     out = jnp.dot(hidden, w_d, preferred_element_type=jnp.float32)
     out = (out * fwd_coef).astype(jnp.bfloat16)
 
     pre_gate = jnp.dot(bwd, w_g, preferred_element_type=jnp.float32)
     pre_up = jnp.dot(bwd, w_u, preferred_element_type=jnp.float32)
-    scaled = (bwd_coef * cot.astype(jnp.float32)).astype(jnp.bfloat16)
-    grad_hidden = contract_last(scaled, w_d)
+    grad_hidden = contract_last(cot, w_d) * bwd_coef
     sigma = jax.nn.sigmoid(pre_gate)
     grad_gate = (grad_hidden * pre_up * sigma * (1.0 + pre_gate * (1.0 - sigma))).astype(
         jnp.bfloat16
     )
     grad_up = (grad_hidden * pre_gate * sigma).astype(jnp.bfloat16)
+    grad_gate, grad_up = lax.optimization_barrier((grad_gate, grad_up))
     total = contract_last(grad_gate, w_g) + contract_last(grad_up, w_u)
     next_input, previous_gradient = scatter(out, total.astype(jnp.bfloat16))
     return (next_input[None], previous_gradient[None])

time: 213 us -> 189 us (0.89)
  matrix products: 55.9 us -> 34.9 us
  other arithmetic: 5.23 us -> 2.14 us
    dot_general x3, matrix products: 29.2 us -> 14.8 us  [contract_last(): lax.dot_general(a, b, (((1,), (1,)), ((), ())), preferred_element_type=jn...]
    dot_general x1, matrix products: 13.2 us -> 5 us  [local(): out = jnp.dot(hidden, w_d, preferred_element_type=jnp.float32)]
    dot_general x0 -> x2, matrix products: none -> 7.84 us  [the longest x1 4.11 us: local(): pre_up = jnp.dot(bwd, w_u, preferred_element_type=jnp.float32)]
    dot_general x1, matrix products: 8.39 us -> 3.78 us  [local(): pre_gate = jnp.dot(bwd, w_g, preferred_element_type=jnp.float32)]
    convert_element_type x1 -> x0, other arithmetic: 3.08 us -> none  [local(): scaled = (bwd_coef * cot.astype(jnp.float32)).astype(jnp.bfloat16)]
    unnamed x12 -> x14, local copies, waits for them, and re-layouts: 5.3 us -> 3.74 us
where the time goes in v2:
time: 189 us; the launch traced here: 188 us
  Pallas kernels  145 us (77%)
  matrix products  34.9 us (18%)
  local copies, waits for them, and re-layouts  5.45 us (3%)
  other arithmetic  2.14 us (1%)
    pallas_call x1, Pallas kernels, gather(): pl.pallas_call(functools.partial(gather_kernel, n_node, n_x, count), out_...  79.7 us
    pallas_call x1, Pallas kernels, scatter(): pl.pallas_call(functools.partial(scatter_kernel, n_section, n_node, n_x,...  65.5 us
    dot_general x3, matrix products, contract_last(): lax.dot_general(a, b, (((1,), (1,)), ((), ())), preferred_element_type=jn...  14.8 us
    dot_general x1, matrix products, local(): out = jnp.dot(hidden, w_d, preferred_element_type=jnp.float32)  5 us
    dot_general x1, matrix products, local(): pre_up = jnp.dot(bwd, w_u, preferred_element_type=jnp.float32)  4.11 us
    dot_general x1, matrix products, local(): pre_gate = jnp.dot(bwd, w_g, preferred_element_type=jnp.float32)  3.78 us

profile of v2, /device:TPU:0, one launch (start us, length us, event | category | flops | bytes accessed | tf_op | source)
XLA Modules:
  0.0 188.4 jit_solution(927129136185337135)
XLA Ops:
  0.6 0.7 select_reduce_fusion.1
  1.4 0.7 select_reduce_fusion
  2.1 0.1 copy.23
  2.2 0.1 copy.22
  2.3 0.7 select_maximum_fusion.refs_0_
  2.9 79.7 %shard_map.113 = (f32[4,4,64,128]{3,2,1,0:T(8,128)}, bf16[4,4,64,2048]{3,2,1,0:T(8,128)(2,1)}, bf16[4,4,64,2048]{3,2,1,0:T(8,128)(2,1)}, bf16[4,4,64,2048]{3,2,1,0:T(8,128)(2,1)}) custom-call(f32[64,128]{1,0:T(8,128)} %select_maximum_fusion.refs_0_, bf16[64,2048]{1,0:T(8,128)(2,1)} %bitcast.53, bf16[64,2048]{1,0:T(8,128)(2,1)} %bitcast.54, ...), custom_call_target="tpu_custom_call" | custom-call | tf_op jit(solution)/shard_map/pallas_call | solution.py:143
  82.6 1.5 constant_dynamic-slice_fusion
  84.2 0.2 copy.27
  84.4 0.2 copy.26
  84.5 0.0 copy-start.1
  84.5 0.0 copy-start.4
  84.5 6.4 %fusion = f32[1024,768]{1,0:T(8,128)S(1)} fusion(bf16[1024,2048]{1,0:T(8,128)(2,1)} %bitcast.69, bf16[1,1,768,2048]{3,2,1,0:T(8,128)(2,1)} %param.19), kind=kOutput, calls=%fused_computation.2 | convolution fusion | flops 3221225472 | bytes 10485760 | tf_op jit(solution)/shard_map/dot_general | solution.py:378
  90.9 0.0 copy-done.1
  90.9 0.0 copy-done.4
  90.9 0.0 copy-start.3
  90.9 3.4 %fusion.6 = f32[1024,768]{1,0:T(8,128)S(1)} fusion(bf16[1024,2048]{1,0:T(8,128)(2,1)S(1)} %bitcast.67, bf16[1,1,2048,768]{3,2,1,0:T(8,128)(2,1)S(1)} %copy-done.4), kind=kOutput, calls=%fused_computation.8 | convolution fusion | flops 3221225472 | bytes 10485760 | tf_op jit(solution)/shard_map/dot_general | solution.py:414
  94.4 0.0 copy-done.3
  94.4 0.0 copy-start.2
  94.4 3.7 %multiply_convert_fusion.3 = bf16[1024,768]{1,0:T(8,128)(2,1)S(1)} fusion(f32[1024,768]{1,0:T(8,128)S(1)} %fusion.6, bf16[1024,2048]{1,0:T(8,128)(2,1)S(1)} %bitcast.68, bf16[1,1,2048,768]{3,2,1,0:T(8,128)(2,1)S(1)} %copy-done.3), kind=kOutput, calls=%fused_computation.19 | convolution fusion | flops 3225944064 | bytes 12058624 | tf_op jit(solution)/shard_map/dot_general | solution.py:413
  98.1 0.0 copy-done.2
  98.2 0.0 copy-start
  98.2 5.0 %multiply_convert_fusion = bf16[1024,2048]{1,0:T(8,128)(2,1)} fusion(bf16[1024,768]{1,0:T(8,128)(2,1)S(1)} %multiply_convert_fusion.3, f32[1024]{0:T(1024)S(1)} %bitcast.60, bf16[1,1,768,2048]{3,2,1,0:T(8,128)(2,1)S(1)} %copy-done.2), kind=kOutput, calls=%fused_computation.1 | convolution fusion | flops 3225419776 | bytes 8916992 | tf_op jit(solution)/shard_map/dot_general | solution.py:417
  103.2 0.0 copy-done
  103.2 3.8 %multiply_convert_fusion.1 = (bf16[1024,768]{1,0:T(8,128)(2,1)S(1)}, f32[1024,768]{1,0:T(8,128)S(1)}) fusion(f32[1024,768]{1,0:T(8,128)S(1)} %fusion, f32[1024]{0:T(1024)S(1)} %bitcast.58, bf16[1024,2048]{1,0:T(8,128)(2,1)S(1)} %bitcast.65, bf16[1,1,2048,768]{3,2,1,0:T(8,128)(2,1)S(1)} %copy-done.3), kind=kOutput, calls=%fused_computation.16 | convolution fusion | flops 3226730496 | bytes 15208448 | tf_op jit(solution)/shard_map/dot_general | solution.py:420
  107.0 4.1 %multiply_convert_fusion.2 = bf16[1024,768]{1,0:T(8,128)(2,1)S(1)} fusion(f32[1024,768]{1,0:T(8,128)S(1)} %get-tuple-element.21, f32[1024,768]{1,0:T(8,128)S(1)} %fusion, bf16[1024,2048]{1,0:T(8,128)(2,1)S(1)} %bitcast.66, bf16[1,1,2048,768]{3,2,1,0:T(8,128)(2,1)S(1)} %copy-done.4, f32[1024]{0:T(1024)S(1)} %bitcast.59), kind=kOutput, calls=%fused_computation.17 | convolution fusion | flops 3229876224 | bytes 15208448 | tf_op jit(solution)/shard_map/dot_general | solution.py:421
  111.1 3.4 %fusion.8 = f32[1024,2048]{1,0:T(8,128)S(1)} fusion(bf16[1024,768]{1,0:T(8,128)(2,1)S(1)} %multiply_convert_fusion.2, bf16[1,1,2048,768]{3,2,1,0:T(8,128)(2,1)S(1)} %copy-done.3), kind=kOutput, calls=%fused_computation.10 | convolution fusion | flops 3221225472 | bytes 13107200 | tf_op jit(solution)/shard_map/dot_general | solution.py:378
  114.5 5.0 %add_convert_fusion = bf16[1024,2048]{1,0:T(8,128)(2,1)} fusion(f32[1024,2048]{1,0:T(8,128)S(1)} %fusion.8, bf16[1024,768]{1,0:T(8,128)(2,1)S(1)} %get-tuple-element.15, bf16[1,1,2048,768]{3,2,1,0:T(8,128)(2,1)S(1)} %copy-done.4), kind=kOutput, calls=%fused_computation | convolution fusion | flops 3225419776 | bytes 17301504 | tf_op jit(solution)/shard_map/dot_general | solution.py:378
  119.6 65.5 %shard_map.114 = (bf16[64,2048]{1,0:T(8,128)(2,1)}, bf16[64,2048]{1,0:T(8,128)(2,1)}) custom-call(bf16[4,2,2,64,2048]{4,3,2,1,0:T(8,128)(2,1)} %bitcast.50, bf16[4,2,2,64,2048]{4,3,2,1,0:T(8,128)(2,1)} %bitcast.51), custom_call_target="tpu_custom_call" | custom-call | tf_op jit(solution)/shard_map/pallas_call | solution.py:345
  185.1 1.7 copy.30
  186.8 1.7 copy.31
Async XLA Ops:
  84.5 6.4 %copy-start.1 = (bf16[4,4,64,2048]{3,2,1,0:T(8,128)(2,1)S(1)}, bf16[4,4,64,2048]{3,2,1,0:T(8,128)(2,1)}, u32[]{:S(2)}) copy-start(bf16[4,4,64,2048]{3,2,1,0:T(8,128)(2,1)} %get-tuple-element.10) | copy-start | bytes 12582916
  84.5 6.4 %copy-start.4 = (bf16[1,1,2048,768]{3,2,1,0:T(8,128)(2,1)S(1)}, bf16[1,1,2048,768]{3,2,1,0:T(8,128)(2,1)}, u32[]{:S(2)}) copy-start(bf16[1,1,2048,768]{3,2,1,0:T(8,128)(2,1)} %param.18) | copy-start | bytes 9437188
  90.9 3.4 %copy-start.3 = (bf16[1,1,2048,768]{3,2,1,0:T(8,128)(2,1)S(1)}, bf16[1,1,2048,768]{3,2,1,0:T(8,128)(2,1)}, u32[]{:S(2)}) copy-start(bf16[1,1,2048,768]{3,2,1,0:T(8,128)(2,1)} %param.17) | copy-start | bytes 9437188
  94.4 3.8 %copy-start.2 = (bf16[1,1,768,2048]{3,2,1,0:T(8,128)(2,1)S(1)}, bf16[1,1,768,2048]{3,2,1,0:T(8,128)(2,1)}, u32[]{:S(2)}) copy-start(bf16[1,1,768,2048]{3,2,1,0:T(8,128)(2,1)} %param.19) | copy-start | bytes 9437188
  98.2 5.0 %copy-start = (bf16[4,4,64,2048]{3,2,1,0:T(8,128)(2,1)S(1)}, bf16[4,4,64,2048]{3,2,1,0:T(8,128)(2,1)}, u32[]{:S(2)}) copy-start(bf16[4,4,64,2048]{3,2,1,0:T(8,128)(2,1)} %get-tuple-element.13) | copy-start | bytes 12582916
